TPU v7x, 32 devices: a whole 2x2x4 slice. The times are simulated.
32 devices in a mesh: dp: 16 (over z, x, core), head: 2 (over y).
Axes of the slice: x: 2, y: 2, z: 4, core: 2. Of those that a mesh axis runs over, the one named last changes fastest.
Arguments:
- tokens: bfloat16 [32768, 512], P(('dp', 'head')), may hold values from -6 to 6
- lengths: int32 [128], P('dp'), may hold values from 40 to 256, as said below
- ln1_gain: float32 [512], replicated, may hold values from 0.5 to 1.5
- ln1_bias: float32 [512], replicated, may hold values from -1 to 1
- w_query: bfloat16 [512, 512], P(None, 'head'), may hold values from -0.25 to 0.25
- w_key: bfloat16 [512, 512], P(None, 'head'), may hold values from -0.25 to 0.25
- w_value: bfloat16 [512, 512], P(None, 'head'), may hold values from -0.25 to 0.25
- w_out: bfloat16 [512, 512], P('head'), may hold values from -1 to 1
- sort_first: bfloat16 [512, 512], replicated, may hold values from -0.25 to 0.25
- sort_second: bfloat16 [512, 8], replicated, may hold values from -0.5 to 0.5
- ln2_gain: float32 [512], replicated, may hold values from 0.5 to 1.5
- ln2_bias: float32 [512], replicated, may hold values from -1 to 1
- w_up: bfloat16 [512, 2048], replicated, may hold values from -0.25 to 0.25
- w_down: bfloat16 [2048, 512], replicated, may hold values from -0.125 to 0.125
- cotangent: bfloat16 [32768, 512], P(('dp', 'head')), may hold values from -6 to 6
Outputs:
- output: bfloat16 [32768, 512], P(('dp', 'head'))
- input_grad: bfloat16 [32768, 512], P(('dp', 'head'))
- grad_ln1_gain: float32 [512], replicated
- grad_ln1_bias: float32 [512], replicated
- grad_query: float32 [512, 512], P(None, 'head')
- grad_key: float32 [512, 512], P(None, 'head')
- grad_value: float32 [512, 512], P(None, 'head')
- grad_out: float32 [512, 512], P('head')
- grad_sort_first: float32 [512, 512], replicated
- grad_sort_second: float32 [512, 8], replicated
- grad_ln2_gain: float32 [512], replicated
- grad_ln2_bias: float32 [512], replicated
- grad_up: float32 [512, 2048], replicated
- grad_down: float32 [2048, 512], replicated
Inputs may be any that keep to these rules, and one draw needn't show every extreme that they name: `lengths`: some sequence has exactly 256 valid tokens and some has exactly 40.
All inputs are finite; a program needn't handle non-finite values.
Results may differ from a plain program's by a relative error of at most 0.017.
Values may be sent and summed in bfloat16 or wider, within the bound.
No kernel may reach another device: no remote copies, remote signals or barrier semaphores. Data moves between devices by JAX's collectives and lax.ppermute only.
A program may use at most 192 MiB of HBM per device.

v0:
```python
import jax
import jax.numpy as jnp
from jax import lax
from jax.sharding import PartitionSpec as P

HD = 64
BL = 32
ITERS = 8
LMAX = 256
precise = lax.Precision.HIGHEST


def smooth_gate(values):
    return jax.nn.gelu(values, approximate=False)


def layer_norm(values, gain_vec, bias_vec):
    center = values - jnp.mean(values, axis=-1, keepdims=True)
    spread = jnp.mean(center * center, axis=-1, keepdims=True)
    return center * lax.rsqrt(spread + 1e-05) * gain_vec + bias_vec


def log_total(values, along):
    row_top = jnp.max(values, axis=along, keepdims=True)
    return row_top + jnp.log(jnp.sum(jnp.exp(values - row_top), axis=along, keepdims=True))


def sort_plan(summary, sort_one, sort_two, block_ok):
    hidden = smooth_gate(jnp.einsum("cid,de->cie", summary, sort_one, precision=precise))
    logits = jnp.einsum("cie,ej->cij", hidden, sort_two, precision=precise)
    diagonal = jnp.eye(logits.shape[1], dtype=jnp.bool_)[None]
    allowed = block_ok[:, :, None] & block_ok[:, None, :] | diagonal & ~block_ok[:, :, None]
    plan_log = jnp.where(allowed, logits, -1e30)
    for sweep_index in range(ITERS):
        plan_log = plan_log - log_total(plan_log, 2)
        plan_log = plan_log - log_total(plan_log, 1)
    return jnp.exp(plan_log)


def outer_product(left, right):
    return lax.dot_general(
        left, right, (((0,), (0,)), ((), ())), preferred_element_type=jnp.float32
    )


def attend_forward(queries, key_rows, value_rows, soft_plan, tok_ok, block_ok):
    tok_mask = tok_ok[..., None, None].astype(jnp.bfloat16)
    key_kept = key_rows * tok_mask
    value_kept = value_rows * tok_mask
    sorted_keys = jnp.einsum(
        "cij,cjthd->cithd", soft_plan, key_kept.astype(jnp.float32), precision=precise
    ).astype(jnp.bfloat16)
    sorted_values = jnp.einsum(
        "cij,cjthd->cithd", soft_plan, value_kept.astype(jnp.float32), precision=precise
    ).astype(jnp.bfloat16)
    all_keys = jnp.concatenate([key_kept, sorted_keys], axis=2)
    all_values = jnp.concatenate([value_kept, sorted_values], axis=2)
    score_scale = queries.shape[-1] ** (-0.5)
    scores = (
        jnp.einsum("cibhd,cikhd->cihbk", queries, all_keys, preferred_element_type=jnp.float32)
        * score_scale
    )
    key_ok = jnp.concatenate([tok_ok, jnp.broadcast_to(block_ok[:, :, None], tok_ok.shape)], axis=2)
    allowed = key_ok[:, :, None, None, :] | ~tok_ok[:, :, None, :, None]
    scores = jnp.where(allowed, scores, -1e30)
    weights = jnp.exp(scores - log_total(scores, 4))
    weights_low = weights.astype(jnp.bfloat16)
    mixed_rows = jnp.einsum(
        "cihbk,cikhd->cibhd", weights_low, all_values, preferred_element_type=jnp.float32
    )
    mixed_rows = mixed_rows * tok_ok[..., None, None].astype(jnp.float32)
    return (mixed_rows, (key_kept, all_keys, all_values, weights, weights_low))


def attend_backward(grad_mixed, queries, soft_plan, tok_ok, saved_state):
    key_kept, all_keys, all_values, weights, weights_low = saved_state
    block_len = key_kept.shape[2]
    score_scale = queries.shape[-1] ** (-0.5)
    value_kept = all_values[:, :, :block_len]
    grad_rows = grad_mixed * tok_ok[..., None, None].astype(jnp.bfloat16)
    grad_weights = jnp.einsum(
        "cibhd,cikhd->cihbk", grad_rows, all_values, preferred_element_type=jnp.float32
    )
    grad_all_values = jnp.einsum(
        "cihbk,cibhd->cikhd", weights_low, grad_rows, preferred_element_type=jnp.float32
    )
    weighted = jnp.sum(weights * grad_weights, axis=4, keepdims=True)
    grad_scores = (weights * (grad_weights - weighted)).astype(jnp.bfloat16)
    grad_queries = (
        jnp.einsum("cihbk,cikhd->cibhd", grad_scores, all_keys, preferred_element_type=jnp.float32)
        * score_scale
    )
    grad_all_keys = (
        jnp.einsum("cihbk,cibhd->cikhd", grad_scores, queries, preferred_element_type=jnp.float32)
        * score_scale
    )
    grad_sorted_keys = grad_all_keys[:, :, block_len:]
    grad_sorted_values = grad_all_values[:, :, block_len:]
    grad_plan = jnp.einsum(
        "cithd,cjthd->cij", grad_sorted_keys, key_kept.astype(jnp.float32), precision=precise
    )
    grad_plan = grad_plan + jnp.einsum(
        "cithd,cjthd->cij", grad_sorted_values, value_kept.astype(jnp.float32), precision=precise
    )
    key_total = grad_all_keys[:, :, :block_len] + jnp.einsum(
        "cij,cithd->cjthd", soft_plan, grad_sorted_keys, precision=precise
    )
    value_total = grad_all_values[:, :, :block_len] + jnp.einsum(
        "cij,cithd->cjthd", soft_plan, grad_sorted_values, precision=precise
    )
    tok_mask = tok_ok[..., None, None].astype(jnp.float32)
    return (
        grad_queries.astype(jnp.bfloat16),
        (key_total * tok_mask).astype(jnp.bfloat16),
        (value_total * tok_mask).astype(jnp.bfloat16),
        grad_plan,
    )


def run_attention(normed_here, span_list, query_cols, key_cols, value_cols, sort_one, sort_two):
    seq_count = span_list.shape[0]
    nblocks = LMAX // BL
    heads_here = query_cols.shape[1] // HD
    positions = jnp.arange(LMAX, dtype=jnp.int32)
    tok_ok = (positions[None, :] < span_list[:, None]).reshape(seq_count, nblocks, BL)
    block_ok = (jnp.arange(nblocks, dtype=jnp.int32) * BL)[None, :] < span_list[:, None]
    block_shape = (seq_count, nblocks, BL, heads_here, HD)
    queries = (
        jnp.dot(normed_here, query_cols, preferred_element_type=jnp.float32)
        .astype(jnp.bfloat16)
        .reshape(block_shape)
    )
    key_rows = (
        jnp.dot(normed_here, key_cols, preferred_element_type=jnp.float32)
        .astype(jnp.bfloat16)
        .reshape(block_shape)
    )
    value_rows = (
        jnp.dot(normed_here, value_cols, preferred_element_type=jnp.float32)
        .astype(jnp.bfloat16)
        .reshape(block_shape)
    )
    summary = jnp.sum(
        normed_here.reshape(seq_count, nblocks, BL, -1).astype(jnp.float32) * tok_ok[..., None],
        axis=2,
    ) * BL ** (-0.5)

    def plan_of(summary_in, first_in, second_in):
        return sort_plan(summary_in, first_in, second_in, block_ok)

    soft_plan, plan_back = jax.vjp(plan_of, summary, sort_one, sort_two)
    mixed_rows, saved_state = attend_forward(
        queries, key_rows, value_rows, soft_plan, tok_ok, block_ok
    )
    mixed_rows = mixed_rows.reshape(normed_here.shape[0], -1).astype(jnp.bfloat16)
    return (mixed_rows, queries, tok_ok, soft_plan, plan_back, saved_state)


def on_device(
    tokens,
    lengths,
    ln1_gain,
    ln1_bias,
    w_query,
    w_key,
    w_value,
    w_out,
    sort_first,
    sort_second,
    ln2_gain,
    ln2_bias,
    w_up,
    w_down,
    cotangent,
):
    head_side = lax.axis_index("head")
    local_rows = tokens.shape[0]
    inputs = tokens.astype(jnp.float32)
    sort_one = sort_first.astype(jnp.float32)
    sort_two = sort_second.astype(jnp.float32)
    normed_f, norm_back = jax.vjp(layer_norm, inputs, ln1_gain, ln1_bias)
    normed = normed_f.astype(jnp.bfloat16)
    normed_here = lax.all_gather(normed, "head", axis=0, tiled=True)
    query_cols, key_cols, value_cols, out_rows = (w_query, w_key, w_value, w_out)
    sort_share = (head_side == 0).astype(jnp.float32)
    mixed_rows, queries, tok_ok, soft_plan, plan_back, saved_state = run_attention(
        normed_here, lengths, query_cols, key_cols, value_cols, sort_one, sort_two
    )
    attention = lax.psum_scatter(
        jnp.dot(mixed_rows, w_out, preferred_element_type=jnp.float32).astype(jnp.bfloat16),
        "head",
        scatter_dimension=0,
        tiled=True,
    ).astype(jnp.float32)
    middle = inputs + attention
    normed_two_f, norm_two_back = jax.vjp(layer_norm, middle, ln2_gain, ln2_bias)
    normed_two = normed_two_f.astype(jnp.bfloat16)
    up_value = jnp.dot(normed_two, w_up, preferred_element_type=jnp.float32)
    hidden_f, gate_back = jax.vjp(smooth_gate, up_value)
    hidden = hidden_f.astype(jnp.bfloat16)
    output = (middle + jnp.dot(hidden, w_down, preferred_element_type=jnp.float32)).astype(
        jnp.bfloat16
    )
    grad_hidden = jnp.dot(cotangent, w_down.T, preferred_element_type=jnp.float32).astype(
        jnp.bfloat16
    )
    grad_upin = gate_back(grad_hidden.astype(jnp.float32))[0].astype(jnp.bfloat16)
    grad_down = outer_product(hidden, cotangent)
    grad_up = outer_product(normed_two, grad_upin)
    grad_middle_norm, grad_gain_two, grad_bias_two = norm_two_back(
        jnp.dot(grad_upin, w_up.T, preferred_element_type=jnp.float32)
    )
    grad_middle = cotangent.astype(jnp.float32) + grad_middle_norm
    grad_attention = grad_middle.astype(jnp.bfloat16)
    grad_attention_here = lax.all_gather(grad_attention, "head", axis=0, tiled=True)
    grad_w_out = outer_product(mixed_rows, grad_attention_here)
    grad_mixed = jnp.dot(
        grad_attention_here, out_rows.T, preferred_element_type=jnp.float32
    ).astype(jnp.bfloat16)
    grad_queries, grad_keys, grad_values, grad_plan = attend_backward(
        grad_mixed.reshape(queries.shape), queries, soft_plan, tok_ok, saved_state
    )
    grad_plan = lax.psum(grad_plan, "head")
    grad_summary, grad_first, grad_second = plan_back(grad_plan)
    rows_here = normed_here.shape[0]
    grad_queries = grad_queries.reshape(rows_here, -1)
    grad_keys = grad_keys.reshape(rows_here, -1)
    grad_values = grad_values.reshape(rows_here, -1)
    grad_spread = (grad_summary[:, :, None, :] * tok_ok[..., None] * BL ** (-0.5)).reshape(
        rows_here, -1
    )
    grad_w_query = outer_product(normed_here, grad_queries)
    grad_w_key = outer_product(normed_here, grad_keys)
    grad_w_value = outer_product(normed_here, grad_values)
    total_term = jnp.dot(grad_queries, w_query.T, preferred_element_type=jnp.float32)
    total_term = total_term + jnp.dot(grad_keys, w_key.T, preferred_element_type=jnp.float32)
    grad_normed = lax.psum_scatter(
        (total_term + jnp.dot(grad_values, w_value.T, preferred_element_type=jnp.float32)).astype(
            jnp.bfloat16
        ),
        "head",
        scatter_dimension=0,
        tiled=True,
    ).astype(jnp.float32)
    grad_normed = grad_normed + lax.dynamic_slice_in_dim(
        grad_spread, head_side * local_rows, local_rows, 0
    )
    grad_w_query, grad_w_key, grad_w_value, grad_w_out = lax.psum(
        (grad_w_query, grad_w_key, grad_w_value, grad_w_out), "dp"
    )
    grad_inputs_norm, grad_gain_one, grad_bias_one = norm_back(grad_normed)
    input_grad = (grad_middle + grad_inputs_norm).astype(jnp.bfloat16)
    summed = lax.psum(
        (
            grad_gain_one,
            grad_bias_one,
            grad_first * sort_share,
            grad_second * sort_share,
            grad_gain_two,
            grad_bias_two,
            grad_up,
            grad_down,
        ),
        ("dp", "head"),
    )
    return (
        output,
        input_grad,
        summed[0],
        summed[1],
        grad_w_query,
        grad_w_key,
        grad_w_value,
        grad_w_out,
        summed[2],
        summed[3],
        summed[4],
        summed[5],
        summed[6],
        summed[7],
    )


def solution(mesh):
    return jax.shard_map(
        on_device,
        mesh=mesh,
        in_specs=(
            P(("dp", "head"), None),
            P("dp"),
            P(),
            P(),
            P(None, "head"),
            P(None, "head"),
            P(None, "head"),
            P("head", None),
            P(),
            P(),
            P(),
            P(),
            P(),
            P(),
            P(("dp", "head"), None),
        ),
        out_specs=(
            P(("dp", "head"), None),
            P(("dp", "head"), None),
            P(),
            P(),
            P(None, "head"),
            P(None, "head"),
            P(None, "head"),
            P("head", None),
            P(),
            P(),
            P(),
            P(),
            P(),
            P(),
        ),
        check_vma=False,
    )
```

profile of v0, /device:TPU:0, one launch (start us, length us, event | category | flops | bytes accessed | tf_op | source)
XLA Modules:
  0.0 688.6 jit_solution(9410272883061867089)
XLA Ops:
  16.0 33.3 %all-gather.3.cloned.1.call-done = bf16[2048,512]{1,0:T(8,128)(2,1)} async-done(((bf16[1024,512]{1,0:T(8,128)(2,1)}), bf16[2048,512]{1,0:T(8,128)(2,1)}) %all-gather.3.cloned.1.call-update) | async-done | bytes 2097168 | tf_op jit(solution)/shard_map/all_gather | solution.py:183
  70.4 4.6 reshape.615
  78.3 4.4 reshape.614
  86.8 4.9 copy_multiply_fusion.1
  107.4 4.4 convert_element_type.198
  115.2 31.9 %reduce-scatter.3.cloned.1.call-done = bf16[1024,512]{1,0:T(8,128)(2,1)} async-done(((bf16[2048,512]{1,0:T(8,128)(2,1)}), bf16[1024,512]{1,0:T(8,128)(2,1)}) %reduce-scatter.3.cloned.1.call-update) | async-done | bytes 1048592 | tf_op jit(solution)/shard_map/reduce_scatter | solution.py:189
  150.6 23.5 %multiply_convert_fusion = (bf16[1024,2048]{1,0:T(8,128)(2,1)}, f32[1024,2048]{1,0:T(8,128)S(1)}, f32[1024,2048]{1,0:T(8,128)}) fusion(bf16[512,2048]{1,0:T(8,128)(2,1)S(1)} %copy-done, bf16[1024,512]{1,0:T(8,128)(2,1)S(1)} %copy-done.26, bf16[1024,512]{1,0:T(8,128)(2,1)S(1)} %copy-done.2, f32[512]{0:T(512)} %param.26, f32[512]{0:T(512)} %param.25, ...), kind=kOutput, calls=%fused_computation.12 | convolution fusion | flops 2287992832 | bytes 25178112 | tf_op jit(solution)/shard_map/dot_general | solution.py:198
  174.0 6.9 %fusion.5 = bf16[1024,2048]{1,0:T(8,128)(2,1)S(1)} fusion(f32[1024,2048]{1,0:T(8,128)S(1)} %get-tuple-element.86, f32[1024,2048]{1,0:T(8,128)} %get-tuple-element.110, bf16[1024,512]{1,0:T(8,128)(2,1)S(1)} %copy-done.36, bf16[2048,512]{1,0:T(8,128)(2,1)S(1)} %copy-done.156), kind=kOutput, calls=%fused_computation.8 | convolution fusion | flops 2181038080 | bytes 24117248 | tf_op jit(solution)/shard_map/dot_general | solution.py:204
  187.3 6.9 %fusion.167 = f32[2048,512]{1,0:T(8,128)} fusion(bf16[1024,2048]{1,0:T(8,128)(2,1)} %get-tuple-element.85, bf16[1024,512]{1,0:T(8,128)(2,1)} %param.29), kind=kOutput, calls=%fused_computation.381 | convolution fusion | flops 2147483648 | bytes 9437184 | tf_op jit(solution)/shard_map/dot_general | solution.py:41
  194.3 4.6 fusion.143
  198.9 21.4 %all-gather.5.cloned.1.call-done = bf16[2048,512]{1,0:T(8,128)(2,1)} async-done(((bf16[1024,512]{1,0:T(8,128)(2,1)}), bf16[2048,512]{1,0:T(8,128)(2,1)}) %all-gather.5.cloned.1.call-update) | async-done | bytes 2097168 | tf_op jit(solution)/shard_map/all_gather | solution.py:215
  227.5 7.2 %multiply_reduce_fusion = (f32[8,8,4,32]{3,2,1,0:T(4,128)S(1)}, f32[8,8,4,32,64]{4,3,2,1,0:T(8,128)S(1)}) fusion(f32[8,8,4,32,64]{4,3,2,1,0:T(8,128)S(1)} %copy-done.4, f32[8,8,4,32]{3,2,1,0:T(4,128)} %bitcast.104, pred[8,8,32,64]{3,2,1,0:T(8,128)(4,1)S(1)} %broadcast_or_fusion, bf16[8,8,64,4,64]{4,1,3,2,0:T(8,128)(2,1)} %copy-done.35, ...), kind=kOutput, calls=%fused_computation.47 | convolution fusion | flops 69722112 | bytes 7536640 | tf_op jit(solution)/shard_map/cibhd,cikhd->cihbk/dot_general | solution.py:81
  234.7 5.8 convolution_bitcast_fusion
  249.8 6.4 fusion.65
  256.2 7.6 %fusion.24 = f32[8,8,32,4,64]{4,1,3,2,0:T(8,128)} fusion(f32[8,8,32,4,64]{4,2,3,1,0:T(8,128)S(1)} %slice.17, f32[8,8,8]{2,1,0:T(8,128)S(1)} %get-tuple-element.88, f32[8,8]{1,0:T(8,128)S(1)} %log_add_fusion.1, f32[8,8]{1,0:T(8,128)S(1)} %log_add_fusion.2), kind=kOutput, calls=%fused_computation.42 | convolution fusion | flops 50332672 | bytes 4196864 | tf_op jit(solution)/shard_map/cij,cithd->cjthd/dot_general | solution.py:105
  275.5 7.2 %fusion.22 = f32[8,8,32,4,64]{4,1,3,2,0:T(8,128)} fusion(f32[8,8,32,4,64]{4,2,3,1,0:T(8,128)S(1)} %slice.19, f32[8,8,8]{2,1,0:T(8,128)S(1)} %get-tuple-element.88, f32[8,8]{1,0:T(8,128)S(1)} %log_add_fusion.1, f32[8,8]{1,0:T(8,128)S(1)} %log_add_fusion.2), kind=kOutput, calls=%fused_computation.40 | convolution fusion | flops 50332672 | bytes 4196864 | tf_op jit(solution)/shard_map/cij,cithd->cjthd/dot_general | solution.py:108
  282.6 5.5 fusion.75
  288.2 7.2 %psum.91 = f32[8,8,8]{2,1,0:T(8,128)S(1)} all-reduce(f32[8,8,8]{2,1,0:T(8,128)S(1)} %fusion.75), channel_id=1, replica_groups=mesh['dp'=16,'head'=2] {'head'}, use_global_device_ids=true, to_apply=%region_44.45 | all-reduce | flops 512 | bytes 4096 | tf_op jit(solution)/shard_map/psum | solution.py:223
  295.4 12.7 %fusion.14 = (bf16[8,8,32,4,64]{4,2,3,1,0:T(8,128)(2,1)S(1)}, bf16[8,8,32,4,64]{4,2,3,1,0:T(8,128)(2,1)}) fusion(f32[8,8,64,4,64]{4,2,3,1,0:T(8,128)} %convolution_bitcast_fusion, f32[8,8,32,4,64]{4,1,3,2,0:T(8,128)} %fusion.22, f32[8,8,32]{2,1,0:T(8,128)S(1)} %get-tuple-element.101, f32[8,8,32,4,64]{4,1,3,2,0:T(8,128)} %fusion.24, ...), kind=kLoop, calls=%fused_computation.28 | loop fusion | flops 3145728 | bytes 10493952 | tf_op jit(solution)/shard_map/convert_element_type | solution.py:115
  346.0 6.3 add_convert_fusion.2
  354.0 10.0 %reduce-scatter.5.cloned.1.call-done = bf16[1024,512]{1,0:T(8,128)(2,1)} async-done(((bf16[2048,512]{1,0:T(8,128)(2,1)}), bf16[1024,512]{1,0:T(8,128)(2,1)}) %reduce-scatter.5.cloned.1.call-update) | async-done | bytes 1048592 | tf_op jit(solution)/shard_map/reduce_scatter | solution.py:237
  367.6 40.3 %all-reduce = (f32[512]{0:T(512)}, f32[512]{0:T(512)}, f32[512,8]{0,1:T(8,128)}, f32[512]{0:T(512)}, f32[512]{0:T(512)}) all-reduce(f32[512]{0:T(512)S(1)} %get-tuple-element.16, f32[512]{0:T(512)S(1)} %get-tuple-element.19, f32[512,8]{0,1:T(8,128)S(1)} %fusion.80, ...), channel_id=1, replica_groups=mesh['dp'=16,'head'=2] {'dp','head'}, use_global_device_ids=true, to_apply=%region_96.97 | all-reduce | flops 6144 | bytes 49152 | tf_op jit(solution)/shard_map/psum | solution.py:253
  411.1 55.9 %all-reduce.8.cloned.1.call-done = (f32[512,256]{1,0:T(8,128)}, f32[512,256]{1,0:T(8,128)}, f32[512,256]{1,0:T(8,128)}, f32[256,512]{1,0:T(8,128)}) async-done(((f32[512,256]{1,0:T(8,128)}, f32[512,256]{1,0:T(8,128)}, f32[512,256]{1,0:T(8,128)}, f32[256,512]{1,0:T(8,128)}), (f32[512,256]{1,0:T(8,128)}, f32[512,256]{1,0:T(8,128)}, f32[512,256]{1,0:T(8,128)}, ...) | async-done | bytes 2097168 | tf_op jit(solution)/shard_map/psum | solution.py:248
  467.0 198.9 %all-reduce.6.cloned.1.call-done = (f32[512,512]{1,0:T(8,128)}, f32[512,2048]{1,0:T(8,128)}, f32[2048,512]{1,0:T(8,128)}) async-done(((f32[512,512]{1,0:T(8,128)}, f32[512,2048]{1,0:T(8,128)}, f32[2048,512]{1,0:T(8,128)}), (f32[512,512]{1,0:T(8,128)}, f32[512,2048]{1,0:T(8,128)}, f32[2048,512]{1,0:T(8,128)})) %all-reduce.6.cloned.1.call-update) | async-done | bytes 9437200 | tf_op jit(solution)/shard_map/psum | solution.py:253
  (524 shorter events, 153.7 us)
Async XLA Ops:
  7.2 143.3 %copy-start = (bf16[512,2048]{1,0:T(8,128)(2,1)S(1)}, bf16[512,2048]{1,0:T(8,128)(2,1)}, u32[]{:S(2)}) copy-start(bf16[512,2048]{1,0:T(8,128)(2,1)} %param.27) | copy-start | bytes 6291460
  7.2 45.0 %copy-start.50 = (bf16[512,512]{1,0:T(8,128)(2,1)S(1)}, bf16[512,512]{1,0:T(8,128)(2,1)}, u32[]{:S(2)}) copy-start(bf16[512,512]{1,0:T(8,128)(2,1)} %param.23) | copy-start | bytes 1572868
  7.2 42.1 %all-gather.3.cloned.1.call-start = ((), (), s32[]{:S(2)}) async-start(), calls=%async_computation.2 | async-start | bytes 3145728 | tf_op jit(solution)/shard_map/all_gather | solution.py:183
  8.9 44.3 %copy-start.149 = (bf16[512,8]{0,1:T(8,128)(2,1)S(1)}, bf16[512,8]{0,1:T(8,128)(2,1)}, u32[]{:S(2)}) copy-start(bf16[512,8]{0,1:T(8,128)(2,1)} %param.24) | copy-start | bytes 24580
  8.9 40.4 %copy-start.68 = (f32[1024]{0:T(1024)}, f32[1024]{0:T(1024)S(1)}, u32[]{:S(2)}) copy-start(f32[1024]{0:T(1024)S(1)} %broadcast_multiply_fusion.1) | copy-start | bytes 12292
  10.6 38.7 %copy-start.111 = (f32[1024]{0:T(1024)}, f32[1024]{0:T(1024)S(1)}, u32[]{:S(2)}) copy-start(f32[1024]{0:T(1024)S(1)} %fusion.45) | copy-start | bytes 12292
  10.6 38.7 %copy-start.107 = (f32[1024]{0:T(1024)}, f32[1024]{0:T(1024)S(1)}, u32[]{:S(2)}) copy-start(f32[1024]{0:T(1024)S(1)} %fusion.127) | copy-start | bytes 12292
  13.3 133.8 %reduce-scatter.3.cloned.1.call-start = ((), (), s32[]{:S(2)}) async-start(), calls=%async_computation.3 | async-start | bytes 3145728 | tf_op jit(solution)/shard_map/reduce_scatter | solution.py:189
  13.5 281.9 %copy-start.48 = (f32[8,8,32]{2,1,0:T(8,128)}, f32[8,8,32]{2,1,0:T(8,128)S(1)}, u32[]{:S(2)}) copy-start(f32[8,8,32]{2,1,0:T(8,128)S(1)} %get-tuple-element.101) | copy-start | bytes 24580
  49.3 18.4 %copy-start.5 = (bf16[2048,512]{1,0:T(8,128)(2,1)S(1)}, bf16[2048,512]{1,0:T(8,128)(2,1)}, u32[]{:S(2)}) copy-start(bf16[2048,512]{1,0:T(8,128)(2,1)} %all-gather.3.cloned.1.call-done) | copy-start | bytes 6291460
  52.6 22.3 %copy-start.52 = (f32[8,8,512]{2,1,0:T(8,128)}, f32[8,8,512]{2,1,0:T(8,128)S(1)}, u32[]{:S(2)}) copy-start(f32[8,8,512]{2,1,0:T(8,128)S(1)} %get-tuple-element.105) | copy-start | bytes 393220
  53.1 21.9 %copy-start.54 = (f32[8,8,512]{2,1,0:T(8,128)}, f32[8,8,512]{2,1,0:T(8,128)S(1)}, u32[]{:S(2)}) copy-start(f32[8,8,512]{2,1,0:T(8,128)S(1)} %fusion.85) | copy-start | bytes 393220
  58.0 16.9 %copy-start.20 = (f32[8,8,8]{2,1,0:T(8,128)}, f32[8,8,8]{2,1,0:T(8,128)S(1)}, u32[]{:S(2)}) copy-start(f32[8,8,8]{2,1,0:T(8,128)S(1)} %get-tuple-element.94) | copy-start | bytes 6148
  61.0 14.0 %copy-start.22 = (f32[8,8,8]{2,1,0:T(8,128)}, f32[8,8,8]{2,1,0:T(8,128)S(1)}, u32[]{:S(2)}) copy-start(f32[8,8,8]{2,1,0:T(8,128)S(1)} %get-tuple-element.92) | copy-start | bytes 6148
  61.6 13.4 %copy-start.46 = (f32[8,8]{1,0:T(8,128)}, f32[8,8]{1,0:T(8,128)S(1)}, u32[]{:S(2)}) copy-start(f32[8,8]{1,0:T(8,128)S(1)} %log_add_fusion.8) | copy-start | bytes 772
  107.4 39.7 %copy-start.2 = (bf16[1024,512]{1,0:T(8,128)(2,1)S(1)}, bf16[1024,512]{1,0:T(8,128)(2,1)}, u32[]{:S(2)}) copy-start(bf16[1024,512]{1,0:T(8,128)(2,1)} %param.15) | copy-start | bytes 3145732
  115.1 105.2 %all-gather.5.cloned.1.call-start = ((), (), s32[]{:S(2)}) async-start(), calls=%async_computation.4 | async-start | bytes 3145728 | tf_op jit(solution)/shard_map/all_gather | solution.py:215
  150.5 33.8 %copy-start.147 = (f32[1024]{0:T(1024)}, f32[1024]{0:T(1024)S(1)}, u32[]{:S(2)}) copy-start(f32[1024]{0:T(1024)S(1)} %fusion.128) | copy-start | bytes 12292
  150.5 23.5 %copy-start.36 = (bf16[1024,512]{1,0:T(8,128)(2,1)S(1)}, bf16[1024,512]{1,0:T(8,128)(2,1)}, u32[]{:S(2)}) copy-start(bf16[1024,512]{1,0:T(8,128)(2,1)} %param.29) | copy-start | bytes 3145732
  150.5 23.5 %copy-start.156 = (bf16[2048,512]{1,0:T(8,128)(2,1)S(1)}, bf16[2048,512]{1,0:T(8,128)(2,1)}, u32[]{:S(2)}) copy-start(bf16[2048,512]{1,0:T(8,128)(2,1)} %param.28) | copy-start | bytes 6291460
  187.0 177.0 %reduce-scatter.5.cloned.1.call-start = ((), (), s32[]{:S(2)}) async-start(), calls=%async_computation.5 | async-start | bytes 3145728 | tf_op jit(solution)/shard_map/reduce_scatter | solution.py:237
  314.3 12.5 %copy-start.24 = (bf16[2048,256]{1,0:T(8,128)(2,1)}, bf16[2048,256]{1,0:T(8,128)(2,1)S(1)}, u32[]{:S(2)}) copy-start(bf16[2048,256]{1,0:T(8,128)(2,1)S(1)} %reshape.619) | copy-start | bytes 3145732
  330.9 136.2 %all-reduce.8.cloned.1.call-start = ((), (), s32[]{:S(2)}) async-start(), calls=%async_computation.7 | async-start | bytes 4194304 | tf_op jit(solution)/shard_map/psum | solution.py:248
  340.5 325.5 %all-reduce.6.cloned.1.call-start = ((), (), s32[]{:S(2)}) async-start(), calls=%async_computation.6 | async-start | bytes 18874368 | tf_op jit(solution)/shard_map/psum | solution.py:253
  (143 other events, 639.9 us)
Sparse Core Ops, SparseCore 0:
  13.4 35.8 all-gather.2
  115.2 31.8 reduce-scatter.2
  187.1 33.1 all-gather.4
  331.0 33.0 reduce-scatter.4
  368.4 98.5 all-reduce.7
  474.6 191.2 all-reduce.5
where the time goes:
time: 695 us; the launch traced here: 689 us
  waiting for transfers between devices  352 us (51%)
  matrix products  137 us (20%)
  local copies, waits for them, and re-layouts  75.9 us (11%)
  other arithmetic  58.7 us (8%)
  blocking collectives  47.5 us (7%)
  between operations  17.1 us (2%)
    psum x1, waiting for transfers between devices, on_device(): lax.psum((grad_gain_one, grad_bias_one, grad_first * sort_share, grad_sec...  199 us
    psum x1, waiting for transfers between devices, on_device(): lax.psum((grad_w_query, grad_w_key, grad_w_value, grad_w_out), 'dp')  55.9 us
    psum x1, blocking collectives, on_device(): lax.psum((grad_gain_one, grad_bias_one, grad_first * sort_share, grad_sec...  40.3 us
    all_gather x1, waiting for transfers between devices, on_device(): normed_here = lax.all_gather(normed, 'head', axis=0, tiled=True)  33.3 us
    reduce_scatter x1, waiting for transfers between devices, on_device(): lax.psum_scatter(jnp.dot(mixed_rows, w_out, preferred_element_type=jnp.fl...  31.9 us
    unnamed x327, local copies, waits for them, and re-layouts  31.9 us
    dot_general x1, matrix products, on_device(): up_value = jnp.dot(normed_two, w_up, preferred_element_type=jnp.float32)  23.5 us
    all_gather x1, waiting for transfers between devices, on_device(): lax.all_gather(grad_attention, 'head', axis=0, tiled=True)  21.4 us
  transfers between devices with their start and end apart: 6, of which 6 were waited for; matrix products, arithmetic and copies ran while one was open for 6% of the time, Pallas kernels for 0%

commit v1 on v0

--- a/solution.py
+++ b/solution.py
@@ -8,6 +8,7 @@
 ITERS = 8
 LMAX = 256
 precise = lax.Precision.HIGHEST
+turn_the_points = lambda z_in: lax.psum(lax.psum(z_in, "head"), "dp")
 
 
 def smooth_gate(values):
@@ -250,7 +251,7 @@
     )
     grad_inputs_norm, grad_gain_one, grad_bias_one = norm_back(grad_normed)
     input_grad = (grad_middle + grad_inputs_norm).astype(jnp.bfloat16)
-    summed = lax.psum(
+    summed = turn_the_points(
         (
             grad_gain_one,
             grad_bias_one,
@@ -260,8 +261,7 @@
             grad_bias_two,
             grad_up,
             grad_down,
-        ),
-        ("dp", "head"),
+        )
     )
     return (
         output,

time: 695 us -> 815 us (1.17)
  waiting for transfers between devices: 352 us -> 419 us
  blocking collectives: 47.5 us -> 78.2 us
  other arithmetic: 58.7 us -> 78.7 us
    psum x1, waiting for transfers between devices: 55.9 us -> 149 us  [on_device(): lax.psum((grad_w_query, grad_w_key, grad_w_value, grad_w_out), 'dp')]
    psum x1, waiting for transfers between devices: 199 us -> 156 us  [turn_the_points = lambda z_in: lax.psum(lax.psum(z_in, 'head'), 'dp')]
    psum x1 -> x2, blocking collectives: 40.3 us -> 70.4 us  [turn_the_points = lambda z_in: lax.psum(lax.psum(z_in, 'head'), 'dp')]
    reduce_scatter x1, waiting for transfers between devices: 10 us -> 26.1 us  [on_device(): lax.psum_scatter((total_term + jnp.dot(grad_values, w_value.T, preferred_...]
    div x16, other arithmetic: 0.09 us -> 10.9 us  [log_total(): jnp.log(jnp.sum(jnp.exp(values - row_top), axis=along, keepdims=True))]
    unnamed x327 -> x289, local copies, waits for them, and re-layouts: 31.9 us -> 41.1 us
  transfers between devices with their start and end apart: 6 -> 6, of which waited for: 6 -> 6; matrix products, arithmetic and copies ran while one was open for 6% -> 11% of each run, Pallas kernels for 0% -> 0%
where the time goes in v1:
time: 815 us; the launch traced here: 808 us
  waiting for transfers between devices  419 us (51%)
  matrix products  136 us (17%)
  other arithmetic  78.7 us (10%)
  local copies, waits for them, and re-layouts  78.2 us (10%)
  blocking collectives  78.2 us (10%)
  between operations  16.7 us (2%)
    psum x1, waiting for transfers between devices, turn_the_points = lambda z_in: lax.psum(lax.psum(z_in, 'head'), 'dp')  156 us
    psum x1, waiting for transfers between devices, on_device(): lax.psum((grad_w_query, grad_w_key, grad_w_value, grad_w_out), 'dp')  149 us
    psum x2, blocking collectives, turn_the_points = lambda z_in: lax.psum(lax.psum(z_in, 'head'), 'dp')  70.4 us
    unnamed x289, local copies, waits for them, and re-layouts  41.1 us
    all_gather x1, waiting for transfers between devices, on_device(): normed_here = lax.all_gather(normed, 'head', axis=0, tiled=True)  34.5 us
    reduce_scatter x1, waiting for transfers between devices, on_device(): lax.psum_scatter(jnp.dot(mixed_rows, w_out, preferred_element_type=jnp.fl...  31.9 us
    reduce_scatter x1, waiting for transfers between devices, on_device(): lax.psum_scatter((total_term + jnp.dot(grad_values, w_value.T, preferred_...  26.1 us
    dot_general x1, matrix products, on_device(): up_value = jnp.dot(normed_two, w_up, preferred_element_type=jnp.float32)  22 us
  transfers between devices with their start and end apart: 6, of which 6 were waited for; matrix products, arithmetic and copies ran while one was open for 11% of the time, Pallas kernels for 0%

profile of v1, /device:TPU:0, one launch (start us, length us, event | category | flops | bytes accessed | tf_op | source)
XLA Modules:
  0.0 807.8 jit_solution(7266030804401634196)
XLA Ops:
  16.0 34.5 %all-gather.3.cloned.1.call-done = bf16[2048,512]{1,0:T(8,128)(2,1)} async-done(((bf16[1024,512]{1,0:T(8,128)(2,1)}), bf16[2048,512]{1,0:T(8,128)(2,1)}) %all-gather.3.cloned.1.call-update) | async-done | bytes 2097168 | tf_op jit(solution)/shard_map/all_gather | solution.py:184
  81.0 4.9 copy_multiply_fusion.1
  101.9 4.4 convert_element_type.198
  109.7 31.9 %reduce-scatter.3.cloned.1.call-done = bf16[1024,512]{1,0:T(8,128)(2,1)} async-done(((bf16[2048,512]{1,0:T(8,128)(2,1)}), bf16[1024,512]{1,0:T(8,128)(2,1)}) %reduce-scatter.3.cloned.1.call-update) | async-done | bytes 1048592 | tf_op jit(solution)/shard_map/reduce_scatter | solution.py:190
  145.1 22.0 %multiply_convert_fusion = (bf16[1024,2048]{1,0:T(8,128)(2,1)}, f32[1024,2048]{1,0:T(8,128)S(1)}, f32[1024,2048]{1,0:T(8,128)}) fusion(bf16[512,2048]{1,0:T(8,128)(2,1)S(1)} %copy-done, bf16[1024,512]{1,0:T(8,128)(2,1)S(1)} %copy-done.26, bf16[1024,512]{1,0:T(8,128)(2,1)S(1)} %copy-done.2, f32[512]{0:T(512)S(1)} %copy-done.137, f32[512]{0:T(512)S(1)} %copy-done.129, ...), kind=kOutput, calls=%fused_computation.12 | convolution fusion | flops 2287992832 | bytes 25178112 | tf_op jit(solution)/shard_map/dot_general | solution.py:199
  167.1 6.7 fusion.5
  180.6 6.9 fusion.167
  187.6 4.7 fusion.143
  192.2 21.3 %all-gather.5.cloned.1.call-done = bf16[2048,512]{1,0:T(8,128)(2,1)} async-done(((bf16[1024,512]{1,0:T(8,128)(2,1)}), bf16[2048,512]{1,0:T(8,128)(2,1)}) %all-gather.5.cloned.1.call-update) | async-done | bytes 2097168 | tf_op jit(solution)/shard_map/all_gather | solution.py:216
  220.7 8.7 %multiply_reduce_fusion = (f32[8,8,4,32]{3,2,1,0:T(4,128)S(1)}, f32[8,8,4,32,64]{4,3,2,1,0:T(8,128)}) fusion(f32[8,8,4,32,64]{4,3,2,1,0:T(8,128)S(1)} %copy-done.7, f32[8,8,4,32]{3,2,1,0:T(4,128)} %bitcast.104, pred[8,8,32,64]{3,2,1,0:T(8,128)(4,1)S(1)} %broadcast_or_fusion, bf16[8,8,64,4,64]{4,1,3,2,0:T(8,128)(2,1)} %copy-done.34, ...), kind=kOutput, calls=%fused_computation.47 | convolution fusion | flops 69722112 | bytes 7536640 | tf_op jit(solution)/shard_map/cibhd,cikhd->cihbk/dot_general | solution.py:82
  229.4 4.4 convolution_bitcast_fusion
  248.9 6.4 fusion.65
  255.4 6.6 fusion.75
  262.0 7.8 psum.147
  312.4 8.7 %fusion.22 = f32[8,8,32,4,64]{4,1,3,2,0:T(8,128)S(1)} fusion(f32[8,8,32,4,64]{4,2,3,1,0:T(8,128)} %copy-done.3, f32[8,8,8]{2,1,0:T(8,128)S(1)} %get-tuple-element.96, f32[8,8]{1,0:T(8,128)S(1)} %copy-done.57, f32[8,8]{1,0:T(8,128)S(1)} %log_add_fusion.2), kind=kOutput, calls=%fused_computation.40 | convolution fusion | flops 50332672 | bytes 4196864 | tf_op jit(solution)/shard_map/cij,cithd->cjthd/dot_general | solution.py:109
  321.1 6.8 fusion.24
  327.9 11.3 %fusion.14 = (bf16[8,8,32,4,64]{4,2,3,1,0:T(8,128)(2,1)S(1)}, bf16[8,8,32,4,64]{4,2,3,1,0:T(8,128)(2,1)}) fusion(f32[8,8,64,4,64]{4,2,3,1,0:T(8,128)} %copy-done.8, f32[8,8,32,4,64]{4,1,3,2,0:T(8,128)S(1)} %fusion.22, f32[8,8,32]{2,1,0:T(8,128)S(1)} %copy-done.43, f32[8,8,32,4,64]{4,1,3,2,0:T(8,128)S(1)} %fusion.24, f32[8,8,64,4,64]{4,2,3,1,0:T(8,128)} %copy-done.11), kind=kLoop, calls=%fused_computation.28 | loop fusion | flops 3145728 | bytes 10493952 | tf_op jit(solution)/shard_map/convert_element_type | solution.py:116
  341.6 4.3 reshape.619
  367.5 156.4 %all-reduce.9.cloned.1.call-done = (f32[512,512]{1,0:T(8,128)}, f32[512,2048]{1,0:T(8,128)}, f32[2048,512]{1,0:T(8,128)}) async-done(((f32[512,512]{1,0:T(8,128)}, f32[512,2048]{1,0:T(8,128)}, f32[2048,512]{1,0:T(8,128)}), (f32[512,512]{1,0:T(8,128)}, f32[512,2048]{1,0:T(8,128)}, f32[2048,512]{1,0:T(8,128)})) %all-reduce.9.cloned.1.call-update) | async-done | bytes 9437200 | tf_op jit(solution)/shard_map/psum | solution.py:11
  525.2 6.3 add_convert_fusion.2
  532.5 26.1 %reduce-scatter.5.cloned.1.call-done = bf16[1024,512]{1,0:T(8,128)(2,1)} async-done(((bf16[2048,512]{1,0:T(8,128)(2,1)}), bf16[1024,512]{1,0:T(8,128)(2,1)}) %reduce-scatter.5.cloned.1.call-update) | async-done | bytes 1048592 | tf_op jit(solution)/shard_map/reduce_scatter | solution.py:238
  562.1 7.1 all-reduce.2
  569.2 63.3 %all-reduce = (f32[512]{0:T(512)}, f32[512]{0:T(512)}, f32[512,8]{0,1:T(8,128)}, f32[512]{0:T(512)}, f32[512]{0:T(512)}) all-reduce(f32[512]{0:T(512)S(1)} %get-tuple-element.68, f32[512]{0:T(512)S(1)} %get-tuple-element.69, f32[512,8]{0,1:T(8,128)S(1)} %get-tuple-element.70, ...), channel_id=1, replica_groups=mesh['dp'=16,'head'=2] {'dp'}, use_global_device_ids=true, to_apply=%region_97.98 | all-reduce | flops 6144 | bytes 49152 | tf_op jit(solution)/shard_map/psum | solution.py:11
  635.8 149.1 %all-reduce.7.cloned.1.call-done = (f32[512,256]{1,0:T(8,128)}, f32[512,256]{1,0:T(8,128)}, f32[512,256]{1,0:T(8,128)}, f32[256,512]{1,0:T(8,128)}, f32[512,512]...) async-done(((f32[512,256]{1,0:T(8,128)}, f32[512,256]{1,0:T(8,128)}, f32[512,256]{1,0:T(8,128)}, f32[256,512]{1,0:T(8,128)}, f32[512,512]{1,0:T(8,128)}, ...) | async-done | bytes 11534352 | tf_op jit(solution)/shard_map/psum | solution.py:249
  (487 shorter events, 180.5 us)
Async XLA Ops:
  7.2 137.9 %copy-start = (bf16[512,2048]{1,0:T(8,128)(2,1)S(1)}, bf16[512,2048]{1,0:T(8,128)(2,1)}, u32[]{:S(2)}) copy-start(bf16[512,2048]{1,0:T(8,128)(2,1)} %param.27) | copy-start | bytes 6291460
  7.2 46.1 %copy-start.44 = (bf16[512,512]{1,0:T(8,128)(2,1)S(1)}, bf16[512,512]{1,0:T(8,128)(2,1)}, u32[]{:S(2)}) copy-start(bf16[512,512]{1,0:T(8,128)(2,1)} %param.23) | copy-start | bytes 1572868
  7.2 43.2 %all-gather.3.cloned.1.call-start = ((), (), s32[]{:S(2)}) async-start(), calls=%async_computation.2 | async-start | bytes 3145728 | tf_op jit(solution)/shard_map/all_gather | solution.py:184
  8.9 45.4 %copy-start.126 = (bf16[512,8]{0,1:T(8,128)(2,1)S(1)}, bf16[512,8]{0,1:T(8,128)(2,1)}, u32[]{:S(2)}) copy-start(bf16[512,8]{0,1:T(8,128)(2,1)} %param.24) | copy-start | bytes 24580
  14.5 127.2 %reduce-scatter.3.cloned.1.call-start = ((), (), s32[]{:S(2)}) async-start(), calls=%async_computation.3 | async-start | bytes 3145728 | tf_op jit(solution)/shard_map/reduce_scatter | solution.py:190
  14.6 52.8 %copy-start.41 = (f32[8,8,32]{2,1,0:T(8,128)}, f32[8,8,32]{2,1,0:T(8,128)S(1)}, u32[]{:S(2)}) copy-start(f32[8,8,32]{2,1,0:T(8,128)S(1)} %get-tuple-element.109) | copy-start | bytes 24580
  15.4 49.1 %copy-start.134 = (pred[8,8]{1,0:T(8,128)(4,1)}, pred[8,8]{1,0:T(8,128)(4,1)S(1)}, u32[]{:S(2)}) copy-start(pred[8,8]{1,0:T(8,128)(4,1)S(1)} %iota_compare_fusion) | copy-start | bytes 196
  15.4 39.1 %copy-start.122 = (pred[8,8]{1,0:T(8,128)(4,1)}, pred[8,8]{1,0:T(8,128)(4,1)S(1)}, u32[]{:S(2)}) copy-start(pred[8,8]{1,0:T(8,128)(4,1)S(1)} %get-tuple-element.111) | copy-start | bytes 196
  15.4 48.6 %copy-start.127 = (pred[8,8]{1,0:T(8,128)(4,1)}, pred[8,8]{1,0:T(8,128)(4,1)S(1)}, u32[]{:S(2)}) copy-start(pred[8,8]{1,0:T(8,128)(4,1)S(1)} %get-tuple-element.112) | copy-start | bytes 196
  101.9 39.7 %copy-start.2 = (bf16[1024,512]{1,0:T(8,128)(2,1)S(1)}, bf16[1024,512]{1,0:T(8,128)(2,1)}, u32[]{:S(2)}) copy-start(bf16[1024,512]{1,0:T(8,128)(2,1)} %param.15) | copy-start | bytes 3145732
  109.6 103.9 %all-gather.5.cloned.1.call-start = ((), (), s32[]{:S(2)}) async-start(), calls=%async_computation.4 | async-start | bytes 3145728 | tf_op jit(solution)/shard_map/all_gather | solution.py:216
  143.3 33.8 %copy-start.118 = (f32[1024]{0:T(1024)}, f32[1024]{0:T(1024)S(1)}, u32[]{:S(2)}) copy-start(f32[1024]{0:T(1024)S(1)} %broadcast_multiply_fusion) | copy-start | bytes 12292
  145.1 32.0 %copy-start.124 = (f32[1024]{0:T(1024)}, f32[1024]{0:T(1024)S(1)}, u32[]{:S(2)}) copy-start(f32[1024]{0:T(1024)S(1)} %fusion.128) | copy-start | bytes 12292
  180.3 343.6 %all-reduce.9.cloned.1.call-start = ((), (), s32[]{:S(2)}) async-start(), calls=%async_computation.7 | async-start | bytes 18874368 | tf_op jit(solution)/shard_map/psum | solution.py:11
  255.4 29.0 %copy-start.67 = (f32[8,8]{1,0:T(8,128)S(1)}, f32[8,8]{1,0:T(8,128)}, u32[]{:S(2)}) copy-start(f32[8,8]{1,0:T(8,128)} %copy-done.66) | copy-start | bytes 772
  255.4 34.6 %copy-start.51 = (f32[8,8]{1,0:T(8,128)S(1)}, f32[8,8]{1,0:T(8,128)}, u32[]{:S(2)}) copy-start(f32[8,8]{1,0:T(8,128)} %copy-done.50) | copy-start | bytes 772
  255.4 37.0 %copy-start.65 = (f32[8,8]{1,0:T(8,128)S(1)}, f32[8,8]{1,0:T(8,128)}, u32[]{:S(2)}) copy-start(f32[8,8]{1,0:T(8,128)} %copy-done.64) | copy-start | bytes 772
  255.4 41.2 %copy-start.47 = (f32[8,8,512]{2,1,0:T(8,128)S(1)}, f32[8,8,512]{2,1,0:T(8,128)}, u32[]{:S(2)}) copy-start(f32[8,8,512]{2,1,0:T(8,128)} %copy-done.46) | copy-start | bytes 393220
  300.9 257.6 %reduce-scatter.5.cloned.1.call-start = ((), (), s32[]{:S(2)}) async-start(), calls=%async_computation.5 | async-start | bytes 3145728 | tf_op jit(solution)/shard_map/reduce_scatter | solution.py:238
  312.3 41.2 %copy-start.20 = (bf16[2048,256]{1,0:T(8,128)(2,1)}, bf16[2048,256]{1,0:T(8,128)(2,1)S(1)}, u32[]{:S(2)}) copy-start(bf16[2048,256]{1,0:T(8,128)(2,1)S(1)} %reshape.617) | copy-start | bytes 3145732
  359.0 426.0 %all-reduce.7.cloned.1.call-start = ((), (), s32[]{:S(2)}) async-start(), calls=%async_computation.6 | async-start | bytes 23068672 | tf_op jit(solution)/shard_map/psum | solution.py:249
  531.5 27.6 %copy-start.63 = (f32[1024]{0:T(1024)S(1)}, f32[1024]{0:T(1024)}, u32[]{:S(2)}) copy-start(f32[1024]{0:T(1024)} %copy-done.62) | copy-start | bytes 12292
  531.5 27.6 %copy-start.120 = (f32[512]{0:T(512)S(1)}, f32[512]{0:T(512)}, u32[]{:S(2)}) copy-start(f32[512]{0:T(512)} %param.17) | copy-start | bytes 6148
  559.8 72.7 %copy-start.99 = (f32[1024]{0:T(1024)S(1)}, f32[1024]{0:T(1024)}, u32[]{:S(2)}) copy-start(f32[1024]{0:T(1024)} %copy-done.98) | copy-start | bytes 12292
  (124 other events, 695.2 us)
Sparse Core Ops, SparseCore 0:
  14.6 35.8 all-gather.2
  109.8 31.8 reduce-scatter.2
  180.4 33.1 all-gather.4
  301.0 222.8 all-reduce.8
  526.7 31.8 reduce-scatter.4
  563.8 221.1 all-reduce.6
